TPU v7x, 128 devices: a whole 4x4x4 slice. The times are simulated.
128 devices in a mesh: blk: 32 (over x, y_hi, z), grp: 4 (over y_lo, core).
Axes of the slice: x: 4, y: 4 (y_hi: 2, y_lo: 2; y = y_hi * 2 + y_lo), z: 4, core: 2. Of those that a mesh axis runs over, the one named last changes fastest.
Arguments:
- amplitudes: bfloat16 [1920, 1920], P('blk'), may hold values from -6 to 6
- hole_panel: bfloat16 [1920, 32, 1920], P(None, 'blk', 'grp'), may hold values from -0.375 to 0.375
- virt_fock: bfloat16 [1920, 1920], replicated, may hold values from -0.125 to 0.125
- irrep_sizes: int32 [8], replicated, may hold values from 1 to 480, 1920 in all
- pair_irreps: int32 [32], P('blk'), may hold values from 0 to 7
Outputs:
- dressed: bfloat16 [1920, 32, 1920], P('grp', 'blk')
Inputs may be any that keep to these rules, and one draw needn't show every extreme that they name: `irrep_sizes`: the 8 entries sum to 1920.
All inputs are finite; a program needn't handle non-finite values.
Results may differ from a plain program's by a relative error of at most 0.0049.
Values may be sent and summed in bfloat16 or wider, within the bound.
A program may use at most 128 MiB of HBM per device.

v0:
```python
import jax
import jax.numpy as jnp
from jax import lax
from jax.sharding import PartitionSpec as P


def irrep_of(positions, block_sizes):
    bounds = jnp.cumsum(block_sizes)[:-1]
    return jnp.sum((positions[:, None] >= bounds[None, :]).astype(jnp.int32), axis=1)


def make_local(n_blk, n_grp):

    def local(amplitudes, hole_panel, virt_fock, irrep_sizes, pair_irreps):
        rows = amplitudes.shape[0]
        virtuals = amplitudes.shape[1]
        quarter = hole_panel.shape[2]
        g = lax.axis_index("grp")
        piece = rows // n_grp
        per = n_blk // n_grp
        perm = []
        for q in range(n_grp):
            for k in range(per):
                for i in range(n_grp):
                    perm.append(((per * q + k) * n_grp + i, (n_grp * k + i) * n_grp + q))
        mine = lax.dynamic_slice_in_dim(amplitudes, g * piece, piece, 0)
        mine = lax.ppermute(mine, ("blk", "grp"), perm)
        t_rows = lax.all_gather(mine, "blk", axis=0, tiled=True)
        labels = irrep_of(jnp.arange(virtuals, dtype=jnp.int32), irrep_sizes)
        panel = lax.all_gather(hole_panel.reshape(virtuals, quarter), "grp", axis=1, tiled=True)
        allowed = jnp.bitwise_xor(labels[:, None], labels[None, :]) == pair_irreps[0]
        masked = jnp.where(allowed, panel, jnp.zeros((), jnp.bfloat16))
        coupled = jnp.dot(t_rows, masked, preferred_element_type=jnp.float32).astype(jnp.bfloat16)
        out = jnp.dot(coupled, virt_fock, preferred_element_type=jnp.float32).astype(jnp.bfloat16)
        return out.reshape(quarter, 1, virtuals)

    return local


def solution(mesh):
    in_specs = (P("blk", None), P(None, "blk", "grp"), P(), P(), P("blk"))
    out_specs = P("grp", "blk", None)
    local = make_local(mesh.shape["blk"], mesh.shape["grp"])
    return jax.shard_map(local, mesh=mesh, in_specs=in_specs, out_specs=out_specs, check_vma=False)
```

profile of v0, /device:TPU:1, one launch (start us, length us, event | category | flops | bytes accessed | tf_op | source)
XLA Modules:
  0.0 186.1 jit_solution(730050720383567158)
XLA Ops:
  6.5 0.0 copy-start
  6.5 0.0 all-gather.7.cloned.1.call-start
  6.5 0.9 copy-done
  7.5 4.9 %collective-permute-start = (bf16[15,1920]{1,0:T(8,128)(2,1)S(1)}, bf16[15,1920]{1,0:T(8,128)(2,1)S(1)}, u32[]{:S(2)}, u32[]{:S(2)}) collective-permute-start(bf16[15,1920]{1,0:T(8,128)(2,1)S(1)} %constant_dynamic-slice_fusion), channel_id=1, source_target_pairs={{0,0},{1,4},{2,8},{3,12},{4,16},{5,20},{6,24},{7,28},{8,32},{9,36}... | collective-permute-start | bytes 172808 | tf_op jit(solution)/shard_map/ppermute | solution.py:27
  12.4 1.8 collective-permute-done
  14.3 0.0 copy-start.1
  14.3 0.6 copy-done.1
  14.9 0.0 all-gather.7.cloned.1.call-update
  14.9 0.0 all-gather.5.cloned.1.call-start
  14.9 0.7 all-gather.5.cloned.1.call-update
  15.7 0.8 reduce-window.4
  17.1 0.1 convert_reduce_fusion
  17.2 73.9 %all-gather.7.cloned.1.call-done = bf16[32,15,1920]{2,1,0:T(8,128)(2,1)} async-done(((bf16[1,15,1920]{2,1,0:T(8,128)(2,1)}), bf16[32,15,1920]{2,1,0:T(8,128)(2,1)}) %all-gather.7.cloned.1.call-update) | async-done | bytes 1843216 | tf_op jit(solution)/shard_map/all_gather | solution.py:28
  91.2 1.8 reshape.20
  93.0 71.4 %all-gather.5.cloned.1.call-done = bf16[1920,1,1920]{0,2,1:T(8,128)(2,1)} async-done(((bf16[1920,1,480]{0,2,1:T(8,128)(2,1)}), bf16[1920,1,1920]{0,2,1:T(8,128)(2,1)}) %all-gather.5.cloned.1.call-update) | async-done | bytes 7372816 | tf_op jit(solution)/shard_map/all_gather | solution.py:30
  164.4 14.8 %fusion.11 = bf16[480,1,1920]{2,0,1:T(8,128)(2,1)} fusion(bf16[1920,1920]{1,0:T(8,128)(2,1)} %param.7, bf16[480,1920]{1,0:T(8,128)(2,1)S(1)} %reshape.20, bf16[1920,1,1920]{0,2,1:T(8,128)(2,1)} %all-gather.5.cloned.1.call-done, s32[]{:T(128)} %bitcast.25, s32[1920]{0:T(1024)S(1)} %convert_reduce_fusion), kind=kOutput, calls=%fused_computation.10 | convolution fusion | flops 7090790400 | bytes 18439684 | tf_op jit(solution)/shard_map/dot_general | solution.py:34
  (2 shorter events, 0.0 us)
Async XLA Ops:
  6.5 0.9 copy-start
  6.5 84.6 %all-gather.7.cloned.1.call-start = ((), (), s32[]{:S(2)}) async-start(), calls=%async_computation.1 | async-start | bytes 2027520 | tf_op jit(solution)/shard_map/all_gather | solution.py:28
  7.5 6.7 %collective-permute-start = (bf16[15,1920]{1,0:T(8,128)(2,1)S(1)}, bf16[15,1920]{1,0:T(8,128)(2,1)S(1)}, u32[]{:S(2)}, u32[]{:S(2)}) collective-permute-start(bf16[15,1920]{1,0:T(8,128)(2,1)S(1)} %constant_dynamic-slice_fusion), channel_id=1, source_target_pairs={{0,0},{1,4},{2,8},{3,12},{4,16},{5,20},{6,24},{7,28},{8,32},{9,36}... | collective-permute-start | bytes 172808 | tf_op jit(solution)/shard_map/ppermute | solution.py:27
  14.3 0.6 copy-start.1
  14.9 149.5 %all-gather.5.cloned.1.call-start = ((), (), s32[]{:S(2)}) async-start(), calls=%async_computation | async-start | bytes 9216000 | tf_op jit(solution)/shard_map/all_gather | solution.py:30
Sparse Core Ops, SparseCore 0:
  15.0 76.1 all-gather.6
  92.8 71.5 all-gather.4
where the time goes:
time: 186 us
  waiting for transfers between devices  148 us (80%)
  matrix products  14.8 us (8%)
  between operations  14.1 us (8%)
  starting transfers between devices  4.98 us (3%)
  local copies, waits for them, and re-layouts  3.4 us (2%)
    all_gather x1, waiting for transfers between devices, local(): t_rows = lax.all_gather(mine, 'blk', axis=0, tiled=True)  73.9 us
    all_gather x1, waiting for transfers between devices, local(): lax.all_gather(hole_panel.reshape(virtuals, quarter), 'grp', axis=1, tile...  71.4 us
    dot_general x1, matrix products, local(): jnp.dot(coupled, virt_fock, preferred_element_type=jnp.float32)  14.8 us
    ppermute x1, starting transfers between devices, local(): mine = lax.ppermute(mine, ('blk', 'grp'), perm)  4.94 us
  transfers between devices with their start and end apart: 3, of which 3 were waited for; matrix products, arithmetic and copies ran while one was open for 1% of the time, Pallas kernels for 0%

commit v1 on v0

--- a/solution.py
+++ b/solution.py
@@ -2,6 +2,15 @@
 import jax.numpy as jnp
 from jax import lax
 from jax.sharding import PartitionSpec as P
+
+
+def recover_words(values, out_dim):
+    return jnp.concatenate(
+        lax.all_to_all(
+            jnp.stack([values] * lax.axis_size("blk")), "blk", split_axis=0, concat_axis=0
+        ),
+        axis=out_dim,
+    )
 
 
 def irrep_of(positions, block_sizes):
@@ -25,7 +34,7 @@
                     perm.append(((per * q + k) * n_grp + i, (n_grp * k + i) * n_grp + q))
         mine = lax.dynamic_slice_in_dim(amplitudes, g * piece, piece, 0)
         mine = lax.ppermute(mine, ("blk", "grp"), perm)
-        t_rows = lax.all_gather(mine, "blk", axis=0, tiled=True)
+        t_rows = recover_words(mine, 0)
         labels = irrep_of(jnp.arange(virtuals, dtype=jnp.int32), irrep_sizes)
         panel = lax.all_gather(hole_panel.reshape(virtuals, quarter), "grp", axis=1, tiled=True)
         allowed = jnp.bitwise_xor(labels[:, None], labels[None, :]) == pair_irreps[0]

time: 186 us -> 129 us (0.69)
  waiting for transfers between devices: 148 us -> 77.4 us
  starting transfers between devices: 4.98 us -> 18.5 us
    all_gather x1 -> x0, waiting for transfers between devices: 73.9 us -> none  [local(): t_rows = lax.all_gather(mine, 'blk', axis=0, tiled=True)]
    all_to_all x0 -> x1, waiting for transfers between devices: none -> 30.8 us  [recover_words(): lax.all_to_all(jnp.stack([values] * lax.axis_size('blk')), 'blk', split_a...]
    all_gather x1, waiting for transfers between devices: 71.4 us -> 44.1 us  [local(): lax.all_gather(hole_panel.reshape(virtuals, quarter), 'grp', axis=1, tile...]
    all_to_all x0 -> x1, starting transfers between devices: none -> 13.5 us  [recover_words(): lax.all_to_all(jnp.stack([values] * lax.axis_size('blk')), 'blk', split_a...]
    unnamed x5 -> x4, local copies, waits for them, and re-layouts: 3.37 us -> 0.22 us
  transfers between devices with their start and end apart: 3 -> 3, of which waited for: 3 -> 3; matrix products, arithmetic and copies ran while one was open for 1% -> 3% of each run, Pallas kernels for 0% -> 0%
where the time goes in v1:
time: 129 us
  waiting for transfers between devices  77.4 us (60%)
  starting transfers between devices  18.5 us (14%)
  matrix products  15.3 us (12%)
  between operations  14.1 us (11%)
  local copies, waits for them, and re-layouts  3.32 us (3%)
    all_gather x1, waiting for transfers between devices, local(): lax.all_gather(hole_panel.reshape(virtuals, quarter), 'grp', axis=1, tile...  44.1 us
    all_to_all x1, waiting for transfers between devices, recover_words(): lax.all_to_all(jnp.stack([values] * lax.axis_size('blk')), 'blk', split_a...  30.8 us
    dot_general x1, matrix products, local(): jnp.dot(coupled, virt_fock, preferred_element_type=jnp.float32)  15.3 us
    all_to_all x1, starting transfers between devices, recover_words(): lax.all_to_all(jnp.stack([values] * lax.axis_size('blk')), 'blk', split_a...  13.5 us
    ppermute x1, starting transfers between devices, local(): mine = lax.ppermute(mine, ('blk', 'grp'), perm)  4.94 us
  transfers between devices with their start and end apart: 3, of which 3 were waited for; matrix products, arithmetic and copies ran while one was open for 3% of the time, Pallas kernels for 0%

profile of v1, /device:TPU:1, one launch (start us, length us, event | category | flops | bytes accessed | tf_op | source)
XLA Modules:
  0.0 128.8 jit_solution(4137564691364419771)
XLA Ops:
  6.5 0.0 copy-start
  6.5 0.0 copy-start.1
  6.5 0.0 all-gather.3.cloned.1.call-start
  6.5 0.7 all-gather.3.cloned.1.call-update
  7.3 0.2 copy-done
  7.5 4.9 %collective-permute-start = (bf16[15,1920]{1,0:T(8,128)(2,1)S(1)}, bf16[15,1920]{1,0:T(8,128)(2,1)S(1)}, u32[]{:S(2)}, u32[]{:S(2)}) collective-permute-start(bf16[15,1920]{1,0:T(8,128)(2,1)S(1)} %constant_dynamic-slice_fusion), channel_id=1, source_target_pairs={{0,0},{1,4},{2,8},{3,12},{4,16},{5,20},{6,24},{7,28},{8,32},{9,36}... | collective-permute-start | bytes 172808 | tf_op jit(solution)/shard_map/ppermute | solution.py:36
  12.4 1.8 %collective-permute-done = bf16[15,1920]{1,0:T(8,128)(2,1)S(1)} collective-permute-done((bf16[15,1920]{1,0:T(8,128)(2,1)S(1)}, bf16[15,1920]{1,0:T(8,128)(2,1)S(1)}, u32[]{:S(2)}, u32[]{:S(2)}) %collective-permute-start) | collective-permute-done | bytes 57632 | tf_op jit(solution)/shard_map/ppermute | solution.py:36
  14.3 1.5 %stack.2 = bf16[32,15,1920]{2,1,0:T(8,128)(2,1)} broadcast(bf16[15,1920]{1,0:T(8,128)(2,1)S(1)} %collective-permute-done), dimensions={1,2} | broadcast | bytes 1900800 | tf_op jit(solution)/shard_map/stack | solution.py:10
  15.7 13.5 %all-to-all-start = ((bf16[32,15,1920]{2,1,0:T(8,128)(2,1)}), bf16[32,15,1920]{2,1,0:T(8,128)(2,1)S(1)}, u32[]{:S(2)}, u32[]{:S(2)}) async-start(bf16[32,15,1920]{2,1,0:T(8,128)(2,1)} %stack.2), calls=%async_computation | async-start | bytes 3932160 | tf_op jit(solution)/shard_map/all_to_all | solution.py:9
  29.3 0.0 copy-done.1
  29.3 0.2 reduce-window.4
  30.1 0.1 convert_reduce_fusion
  30.2 30.8 %all-to-all-done = bf16[32,15,1920]{2,1,0:T(8,128)(2,1)S(1)} async-done(((bf16[32,15,1920]{2,1,0:T(8,128)(2,1)}), bf16[32,15,1920]{2,1,0:T(8,128)(2,1)S(1)}, u32[]{:S(2)}, u32[]{:S(2)}) %all-to-all-start) | async-done | bytes 1843232 | tf_op jit(solution)/shard_map/all_to_all | solution.py:9
  61.0 1.6 %reshape.20 = bf16[480,1920]{1,0:T(8,128)(2,1)} reshape(bf16[32,15,1920]{2,1,0:T(8,128)(2,1)S(1)} %all-to-all-done) | data formatting | bytes 3686400 | tf_op jit(solution)/shard_map/reshape | solution.py:8
  62.6 44.1 %all-gather.3.cloned.1.call-done = bf16[1920,1,1920]{0,2,1:T(8,128)(2,1)} async-done(((bf16[1920,1,480]{0,2,1:T(8,128)(2,1)}), bf16[1920,1,1920]{0,2,1:T(8,128)(2,1)}) %all-gather.3.cloned.1.call-update) | async-done | bytes 7372816 | tf_op jit(solution)/shard_map/all_gather | solution.py:39
  106.7 15.3 %fusion.11 = bf16[480,1,1920]{2,0,1:T(8,128)(2,1)} fusion(bf16[1920,1920]{1,0:T(8,128)(2,1)} %param.7, bf16[480,1920]{1,0:T(8,128)(2,1)} %reshape.20, bf16[1920,1,1920]{0,2,1:T(8,128)(2,1)} %all-gather.3.cloned.1.call-done, s32[]{:T(128)} %bitcast.24, s32[1920]{0:T(1024)S(1)} %convert_reduce_fusion), kind=kOutput, calls=%fused_computation.10 | convolution fusion | flops 7090790400 | bytes 18439684 | tf_op jit(solution)/shard_map/dot_general | solution.py:43
  (2 shorter events, 0.0 us)
Async XLA Ops:
  6.5 0.9 copy-start
  6.5 22.7 %copy-start.1 = (s32[8]{0:T(128)S(1)}, s32[8]{0:T(128)}, u32[]{:S(2)}) copy-start(s32[8]{0:T(128)} %param.8) | copy-start | bytes 100
  6.5 100.2 %all-gather.3.cloned.1.call-start = ((), (), s32[]{:S(2)}) async-start(), calls=%async_computation.1 | async-start | bytes 9216000 | tf_op jit(solution)/shard_map/all_gather | solution.py:39
  7.5 6.7 %collective-permute-start = (bf16[15,1920]{1,0:T(8,128)(2,1)S(1)}, bf16[15,1920]{1,0:T(8,128)(2,1)S(1)}, u32[]{:S(2)}, u32[]{:S(2)}) collective-permute-start(bf16[15,1920]{1,0:T(8,128)(2,1)S(1)} %constant_dynamic-slice_fusion), channel_id=1, source_target_pairs={{0,0},{1,4},{2,8},{3,12},{4,16},{5,20},{6,24},{7,28},{8,32},{9,36}... | collective-permute-start | bytes 172808 | tf_op jit(solution)/shard_map/ppermute | solution.py:36
  15.7 45.3 %all-to-all-start = ((bf16[32,15,1920]{2,1,0:T(8,128)(2,1)}), bf16[32,15,1920]{2,1,0:T(8,128)(2,1)S(1)}, u32[]{:S(2)}, u32[]{:S(2)}) async-start(bf16[32,15,1920]{2,1,0:T(8,128)(2,1)} %stack.2), calls=%async_computation | async-start | bytes 3932160 | tf_op jit(solution)/shard_map/all_to_all | solution.py:9
Sparse Core Ops, SparseCore 0:
  9.0 97.6 all-gather.2
